TPU v7x, 32 devices: a whole 2x2x4 slice. The times are simulated.
32 devices in a mesh: rep: 8 (over y, x, core), own: 4 (over z).
Axes of the slice: x: 2, y: 2, z: 4, core: 2. Of those that a mesh axis runs over, the one named last changes fastest.
Arguments:
- gradients: bfloat16 [8, 4, 4, 256, 256], P('rep', 'own')
- owner_index: int32 [4], replicated, may hold values from 0 to 3, as said below
- left_stats: float32 [8, 256, 256], P('own'), as said below
- right_stats: float32 [8, 256, 256], P('own'), as said below
- left_roots: bfloat16 [8, 256, 256], P('own'), as said below
- right_roots: bfloat16 [8, 256, 256], P('own'), as said below
- first_moment: float32 [8, 256, 256], P('own')
- second_moment: float32 [8, 256, 256], P('own'), may hold values from 0.05 to 5
- master: float32 [8, 256, 256], P('own'), may hold values from -6 to 6
Outputs:
- new_left: float32 [8, 256, 256], P('own')
- new_right: float32 [8, 256, 256], P('own')
- new_first: float32 [8, 256, 256], P('own')
- new_second: float32 [8, 256, 256], P('own')
- weights: bfloat16 [4, 256, 256], P(None, 'rep')
Inputs may be any that keep to these rules, and one draw needn't show every extreme that they name: `owner_index`: exactly one owner holds 2 blocks, exactly one holds none, every other holds one. `left_stats`: each matrix is symmetric; every diagonal entry exceeds the sum of the magnitudes of the other entries of its row. `right_stats`: each matrix is symmetric; every diagonal entry exceeds the sum of the magnitudes of the other entries of its row. `left_roots`: each matrix is symmetric. `right_roots`: each matrix is symmetric.
All inputs are finite; a program needn't handle non-finite values.
Results may differ from a plain program's by a relative error of at most 0.001.
Values may be sent and summed in bfloat16 or wider, within the bound.
A program may use at most 64 MiB of HBM per device.

v0:
```python
import jax
import jax.numpy as jnp
from jax import lax
from jax.sharding import PartitionSpec as P

NEWTON = 4
stat_decay = 0.95
first_decay = 0.9
second_decay = 0.99
learning_rate = 0.5


def product(first_factor, second_factor):
    return jnp.matmul(first_factor, second_factor, precision=lax.Precision.HIGHEST)


def destinations(owner_index, capacity):
    block_count = owner_index.shape[0]
    positions = jnp.arange(block_count, dtype=jnp.int32)
    same_owner = owner_index[:, None] == owner_index[None, :]
    earlier = positions[None, :] < positions[:, None]
    ranking = jnp.sum((same_owner & earlier).astype(jnp.int32), axis=1)
    return owner_index * capacity + ranking


def inverse_root(statistic, initial):
    current = initial
    for iteration in range(NEWTON):
        square = product(current, current)
        fourth = product(square, square)
        residual = product(fourth, statistic)
        current = (5.0 * current - product(current, residual)) / 4.0
    return current


def local(
    gradients,
    owner_index,
    left_stats,
    right_stats,
    left_roots,
    right_roots,
    first_moment,
    second_moment,
    master,
):
    capacity = left_stats.shape[0]
    block_size = left_stats.shape[-1]
    block_count = owner_index.shape[0]
    owner_count = lax.axis_size("own")
    slot_total = owner_count * capacity
    destination = destinations(owner_index, capacity)
    placement = destination[None, :] == jnp.arange(slot_total, dtype=jnp.int32)[:, None]
    occupied = jnp.any(placement, axis=1)
    source_block = jnp.sum(
        placement.astype(jnp.int32) * jnp.arange(block_count, dtype=jnp.int32)[None, :], axis=1
    )
    local_blocks = gradients.reshape(block_count, block_size, block_size)
    own_position = lax.axis_index("own")
    occupied_here = lax.dynamic_slice_in_dim(occupied, own_position * capacity, capacity)
    slot_terms = jnp.where(
        occupied[:, None, None], local_blocks[source_block].astype(jnp.float32), 0.0
    )
    owned_partial = lax.psum_scatter(slot_terms, "own", scatter_dimension=0, tiled=True)
    summed = lax.psum(owned_partial, "rep")
    transposed = jnp.swapaxes(summed, 1, 2)
    left_new = stat_decay * left_stats + (1.0 - stat_decay) / block_size * product(
        summed, transposed
    )
    right_new = stat_decay * right_stats + (1.0 - stat_decay) / block_size * product(
        transposed, summed
    )
    statistics = jnp.concatenate([left_new, right_new], axis=0)
    starting = jnp.concatenate([left_roots, right_roots], axis=0).astype(jnp.float32)
    roots = inverse_root(statistics, starting)
    left_root = roots[:capacity]
    right_root = roots[capacity:]
    first_new = first_decay * first_moment + (1.0 - first_decay) * summed
    second_new = second_decay * second_moment + (1.0 - second_decay) * summed * summed
    adam_step = first_new / (jnp.sqrt(second_new) + 1e-08)
    precond = product(product(left_root, summed), right_root)
    graft = jnp.sqrt(jnp.sum(adam_step * adam_step, axis=(1, 2))) / (
        jnp.sqrt(jnp.sum(precond * precond, axis=(1, 2))) + 1e-06
    )
    updated = (master - learning_rate * graft[:, None, None] * precond).astype(jnp.bfloat16)
    row_count = block_size // lax.axis_size("rep")
    row_piece = lax.dynamic_slice_in_dim(updated, lax.axis_index("rep") * row_count, row_count, 1)
    gathered = lax.all_gather(row_piece, "own", axis=0, tiled=True)
    weights = gathered[destination]
    keep_slot = occupied_here[:, None, None]
    new_left = jnp.where(keep_slot, left_new, left_stats)
    new_right = jnp.where(keep_slot, right_new, right_stats)
    new_first = jnp.where(keep_slot, first_new, first_moment)
    new_second = jnp.where(keep_slot, second_new, second_moment)
    return (new_left, new_right, new_first, new_second, weights)


def solution(mesh):
    return jax.shard_map(
        local,
        mesh=mesh,
        in_specs=(
            P("rep", "own", None, None, None),
            P(),
            P("own", None, None),
            P("own", None, None),
            P("own", None, None),
            P("own", None, None),
            P("own", None, None),
            P("own", None, None),
            P("own", None, None),
        ),
        out_specs=(
            P("own", None, None),
            P("own", None, None),
            P("own", None, None),
            P("own", None, None),
            P(None, "rep", None),
        ),
        check_vma=False,
    )
```

profile of v0, /device:TPU:0, one launch (start us, length us, event | category | flops | bytes accessed | tf_op | source)
XLA Modules:
  0.0 161.0 jit_solution(4762941962667526766)
XLA Ops:
  7.2 0.0 copy-start
  7.2 0.0 reduce-scatter.2.cloned.1.call-start
  7.2 0.9 convert_reduce_fusion
  8.1 0.7 compare_select_fusion
  8.8 0.1 fusion.28
  8.9 0.1 select_reduce_fusion
  9.0 0.0 copy-done
  9.0 0.6 gather_fusion
  9.6 0.0 copy-start.5
  9.6 1.6 %convert_select_fusion = f32[8,256,256]{2,1,0:T(8,128)} fusion(bf16[8,256,256]{2,1,0:T(8,128)(2,1)S(1)} %gather_fusion, pred[8]{0:T(512)(128)(4,1)S(1)} %fusion.28), kind=kLoop, calls=%fused_computation.2 | loop fusion | flops 1048576 | bytes 3145736 | tf_op jit(solution)/shard_map/jit(_where)/select_n | solution.py:61
  11.2 0.0 copy-start.6
  11.2 0.0 reduce-scatter.2.cloned.1.call-update
  11.3 0.0 all-reduce.2.cloned.1.call-start
  11.3 0.1 dynamic_slice.6
  11.4 0.0 copy-done.5
  11.4 0.8 copy-done.6
  12.2 0.3 fusion.42
  12.5 45.3 %reduce-scatter.2.cloned.1.call-done = f32[2,256,256]{2,1,0:T(8,128)} async-done(((f32[8,256,256]{2,1,0:T(8,128)}), f32[2,256,256]{2,1,0:T(8,128)}) %reduce-scatter.2.cloned.1.call-update) | async-done | bytes 524304 | tf_op jit(solution)/shard_map/reduce_scatter | solution.py:64
  57.8 0.0 all-reduce.2.cloned.1.call-update
  57.8 1.1 fusion.43
  58.9 0.0 copy-start.2
  59.0 0.0 copy-start.3
  59.0 56.0 %all-reduce.2.cloned.1.call-done = f32[2,256,256]{2,1,0:T(8,128)} async-done(((f32[2,256,256]{2,1,0:T(8,128)}), f32[2,256,256]{2,1,0:T(8,128)}) %all-reduce.2.cloned.1.call-update) | async-done | bytes 524304 | tf_op jit(solution)/shard_map/psum | solution.py:65
  114.9 2.1 %fusion.2 = f32[2,256,256]{2,1,0:T(8,128)S(1)} fusion(f32[2,256,256]{2,1,0:T(8,128)} %all-reduce.2.cloned.1.call-done, f32[2,256,256]{2,1,0:T(8,128)} %param.11), kind=kOutput, calls=%fused_computation.11 | convolution fusion | flops 403046400 | bytes 1572864 | tf_op jit(solution)/shard_map/dot_general | solution.py:14
  117.1 0.0 copy-done.2
  117.1 0.0 copy-done.3
  117.1 0.0 copy-done.1
  117.1 0.0 copy-done.4
  117.1 3.7 %multiply_reduce_fusion.1 = (f32[2]{0:T(128)S(1)}, f32[2,256,256]{2,1,0:T(8,128)}, f32[2,256,256]{2,1,0:T(8,128)}, f32[2,256,256]{2,1,0:T(8,128)}, f32[2,256,256]{2,1,0:T(8,128)}, /*index=5*/f32[2,256,256]{2,1,0:T(8,128)S(1)}) fusion(f32[2,256,256]{2,1,0:T(8,128)S(1)} %copy-done.1, f32[2,256,256]{2,1,0:T(8,128)S(1)} %copy-done.3, ...), kind=kOutput, calls=%fused_computation.33 | convolution fusion | flops 405012480 | bytes 5767178 | tf_op jit(solution)/shard_map/dot_general | solution.py:14
  120.8 1.1 fusion.24
  122.0 0.7 convolution_subtract_fusion.3
  122.7 1.2 fusion.10
  123.9 1.1 fusion.44
  125.1 1.1 fusion.23
  126.3 1.2 convolution_subtract_fusion.2
  127.5 1.2 fusion.7
  128.7 1.3 fusion.45
  130.0 1.1 fusion.22
  131.2 1.2 convolution_subtract_fusion.1
  132.4 1.2 fusion.4
  133.6 1.1 fusion.46
  134.8 1.1 fusion.21
  135.9 1.3 fusion
  137.2 0.7 fusion.47
  137.9 0.8 multiply_reduce_fusion
  138.7 0.9 fusion.27
  139.6 13.3 %all_gather.3 = bf16[8,32,256]{2,1,0:T(8,128)(2,1)S(1)} all-gather(bf16[2,32,256]{2,1,0:T(8,128)(2,1)S(1)} %fusion.27), channel_id=1, replica_groups=mesh['rep'=8,'own'=4] {'own'}, dimensions={0}, use_global_device_ids=true | all-gather | bytes 163840 | tf_op jit(solution)/shard_map/all_gather | solution.py:88
  152.9 1.2 gather_fusion.1
  (8 shorter events, 0.1 us)
Async XLA Ops:
  7.2 1.8 %copy-start = (bf16[1,1,4,256,256]{4,3,2,1,0:T(8,128)(2,1)S(1)}, bf16[1,1,4,256,256]{4,3,2,1,0:T(8,128)(2,1)}, u32[]{:S(2)}) copy-start(bf16[1,1,4,256,256]{4,3,2,1,0:T(8,128)(2,1)} %param.9) | copy-start | bytes 1572868
  7.2 50.6 %reduce-scatter.2.cloned.1.call-start = ((), (), s32[]{:S(2)}) async-start(), calls=%async_computation.1 | async-start | bytes 2621440 | tf_op jit(solution)/shard_map/reduce_scatter | solution.py:64
  9.6 1.8 %copy-start.5 = (bf16[2,256,256]{2,1,0:T(8,128)(2,1)S(1)}, bf16[2,256,256]{2,1,0:T(8,128)(2,1)}, u32[]{:S(2)}) copy-start(bf16[2,256,256]{2,1,0:T(8,128)(2,1)} %param.13) | copy-start | bytes 786436
  11.2 0.9 copy-start.6
  11.3 103.7 %all-reduce.2.cloned.1.call-start = ((), (), s32[]{:S(2)}) async-start(), calls=%async_computation.2 | async-start | bytes 1048576 | tf_op jit(solution)/shard_map/psum | solution.py:65
  58.9 58.2 %copy-start.2 = (f32[2,256,256]{2,1,0:T(8,128)S(1)}, f32[2,256,256]{2,1,0:T(8,128)}, u32[]{:S(2)}) copy-start(f32[2,256,256]{2,1,0:T(8,128)} %param.11) | copy-start | bytes 1572868
  59.0 58.2 %copy-start.3 = (f32[2,256,256]{2,1,0:T(8,128)S(1)}, f32[2,256,256]{2,1,0:T(8,128)}, u32[]{:S(2)}) copy-start(f32[2,256,256]{2,1,0:T(8,128)} %param.15) | copy-start | bytes 1572868
  114.9 2.2 %copy-start.1 = (f32[2,256,256]{2,1,0:T(8,128)S(1)}, f32[2,256,256]{2,1,0:T(8,128)}, u32[]{:S(2)}) copy-start(f32[2,256,256]{2,1,0:T(8,128)} %all-reduce.2.cloned.1.call-done) | copy-start | bytes 1572868
  114.9 2.2 %copy-start.4 = (f32[2,256,256]{2,1,0:T(8,128)S(1)}, f32[2,256,256]{2,1,0:T(8,128)}, u32[]{:S(2)}) copy-start(f32[2,256,256]{2,1,0:T(8,128)} %param.16) | copy-start | bytes 1572868
Sparse Core Ops, SparseCore 0:
  11.4 46.3 reduce-scatter.1
  60.9 54.0 all-reduce.1
where the time goes:
time: 161 us
  waiting for transfers between devices  101 us (63%)
  matrix products  25 us (16%)
  between operations  14.3 us (9%)
  blocking collectives  13.3 us (8%)
  other arithmetic  4.32 us (3%)
  local copies, waits for them, and re-layouts  2.7 us (2%)
    psum x1, waiting for transfers between devices, local(): summed = lax.psum(owned_partial, 'rep')  56 us
    reduce_scatter x1, waiting for transfers between devices, local(): lax.psum_scatter(slot_terms, 'own', scatter_dimension=0, tiled=True)  45.3 us
    dot_general x20, matrix products, product(): jnp.matmul(first_factor, second_factor, precision=lax.Precision.HIGHEST)  25 us
    all_gather x1, blocking collectives, local(): gathered = lax.all_gather(row_piece, 'own', axis=0, tiled=True)  13.3 us
  transfers between devices with their start and end apart: 2, of which 2 were waited for; matrix products, arithmetic and copies ran while one was open for 1% of the time, Pallas kernels for 0%

commit v1 on v0

--- a/solution.py
+++ b/solution.py
@@ -62,7 +62,7 @@
         occupied[:, None, None], local_blocks[source_block].astype(jnp.float32), 0.0
     )
     owned_partial = lax.psum_scatter(slot_terms, "own", scatter_dimension=0, tiled=True)
-    summed = lax.psum(owned_partial, "rep")
+    summed = jnp.sum(lax.all_gather(owned_partial, "rep"), axis=0)
     transposed = jnp.swapaxes(summed, 1, 2)
     left_new = stat_decay * left_stats + (1.0 - stat_decay) / block_size * product(
         summed, transposed

time: 161 us -> 143 us (0.89)
  waiting for transfers between devices: 101 us -> 82.6 us
  other arithmetic: 4.32 us -> 6.89 us
  matrix products: 25 us -> 22.5 us
    psum x1 -> x0, waiting for transfers between devices: 56 us -> none  [local(): summed = lax.psum(owned_partial, 'rep')]
    all_gather x0 -> x1, waiting for transfers between devices: none -> 36.1 us  [local(): summed = jnp.sum(lax.all_gather(owned_partial, 'rep'), axis=0)]
    reduce_sum x0 -> x1, other arithmetic: none -> 2.57 us  [local(): summed = jnp.sum(lax.all_gather(owned_partial, 'rep'), axis=0)]
    dot_general x20, matrix products: 25 us -> 22.5 us  [product(): jnp.matmul(first_factor, second_factor, precision=lax.Precision.HIGHEST)]
where the time goes in v1:
time: 143 us; the launch traced here: 142 us
  waiting for transfers between devices  82.6 us (58%)
  matrix products  22.5 us (16%)
  between operations  14.3 us (10%)
  blocking collectives  13.4 us (9%)
  other arithmetic  6.89 us (5%)
  local copies, waits for them, and re-layouts  2.55 us (2%)
    reduce_scatter x1, waiting for transfers between devices, local(): lax.psum_scatter(slot_terms, 'own', scatter_dimension=0, tiled=True)  46.5 us
    all_gather x1, waiting for transfers between devices, local(): summed = jnp.sum(lax.all_gather(owned_partial, 'rep'), axis=0)  36.1 us
    dot_general x20, matrix products, product(): jnp.matmul(first_factor, second_factor, precision=lax.Precision.HIGHEST)  22.5 us
    all_gather x1, blocking collectives, local(): gathered = lax.all_gather(row_piece, 'own', axis=0, tiled=True)  13.4 us
  transfers between devices with their start and end apart: 2, of which 2 were waited for; matrix products, arithmetic and copies ran while one was open for 1% of the time, Pallas kernels for 0%

profile of v1, /device:TPU:0, one launch (start us, length us, event | category | flops | bytes accessed | tf_op | source)
XLA Modules:
  0.0 142.3 jit_solution(1066943639937398056)
XLA Ops:
  7.2 0.0 copy-start
  7.2 0.0 reduce-scatter.2.cloned.1.call-start
  7.2 0.9 convert_reduce_fusion
  8.1 0.7 compare_select_fusion
  8.8 0.1 fusion.28
  8.9 0.1 select_reduce_fusion
  9.0 0.0 copy-done
  9.0 0.6 gather_fusion
  9.6 1.6 %convert_select_fusion = f32[8,256,256]{2,1,0:T(8,128)} fusion(bf16[8,256,256]{2,1,0:T(8,128)(2,1)S(1)} %gather_fusion, pred[8]{0:T(512)(128)(4,1)S(1)} %fusion.28), kind=kLoop, calls=%fused_computation.2 | loop fusion | flops 1048576 | bytes 3145736 | tf_op jit(solution)/shard_map/jit(_where)/select_n | solution.py:61
  11.2 0.0 reduce-scatter.2.cloned.1.call-update
  11.3 0.0 all-gather.3.cloned.1.call-start
  11.3 46.5 %reduce-scatter.2.cloned.1.call-done = f32[2,256,256]{2,1,0:T(8,128)} async-done(((f32[8,256,256]{2,1,0:T(8,128)}), f32[2,256,256]{2,1,0:T(8,128)}) %reduce-scatter.2.cloned.1.call-update) | async-done | bytes 524304 | tf_op jit(solution)/shard_map/reduce_scatter | solution.py:64
  57.8 0.0 all-gather.3.cloned.1.call-update
  57.8 0.1 dynamic_slice.6
  57.9 0.0 copy-done.5
  57.9 0.0 copy-done.6
  57.9 0.3 fusion.42
  58.2 1.1 fusion.43
  59.4 36.1 %all-gather.3.cloned.1.call-done = f32[16,256,256]{2,1,0:T(8,128)} async-done(((f32[2,256,256]{2,1,0:T(8,128)}), f32[16,256,256]{2,1,0:T(8,128)}) %all-gather.3.cloned.1.call-update) | async-done | bytes 4194320 | tf_op jit(solution)/shard_map/all_gather | solution.py:65
  95.5 2.6 %reduce_sum.50 = f32[2,256,256]{2,1,0:T(8,128)S(1)} reduce(f32[8,2,256,256]{3,2,1,0:T(8,128)} %bitcast.33, f32[]{:T(128)} %constant.15.clone.1), dimensions={0}, to_apply=%region_4.5 | reduce | flops 917504 | bytes 4718596 | tf_op jit(solution)/shard_map/reduce_sum | solution.py:65
  98.1 0.0 copy-done.1
  98.1 0.0 copy-start.2
  98.1 0.0 copy-start.3
  98.1 0.0 copy-start.4
  98.1 0.7 fusion.2
  98.8 0.3 copy-done.2
  99.1 0.2 copy-done.3
  99.3 0.2 copy-done.4
  99.4 2.7 %multiply_reduce_fusion.1 = (f32[2]{0:T(128)S(1)}, f32[2,256,256]{2,1,0:T(8,128)}, f32[2,256,256]{2,1,0:T(8,128)}, f32[2,256,256]{2,1,0:T(8,128)}, f32[2,256,256]{2,1,0:T(8,128)}, /*index=5*/f32[2,256,256]{2,1,0:T(8,128)S(1)}) fusion(f32[2,256,256]{2,1,0:T(8,128)S(1)} %reduce_sum.50, f32[2,256,256]{2,1,0:T(8,128)S(1)} %copy-done.2, ...), kind=kOutput, calls=%fused_computation.33 | convolution fusion | flops 405012480 | bytes 5767178 | tf_op jit(solution)/shard_map/dot_general | solution.py:14
  102.1 1.1 fusion.24
  103.3 0.8 convolution_subtract_fusion.3
  104.0 1.2 fusion.10
  105.2 1.1 fusion.44
  106.4 1.1 fusion.23
  107.5 1.2 convolution_subtract_fusion.2
  108.8 1.2 fusion.7
  110.0 1.3 fusion.45
  111.3 1.1 fusion.22
  112.5 1.2 convolution_subtract_fusion.1
  113.7 1.2 fusion.4
  114.9 1.1 fusion.46
  116.1 1.1 fusion.21
  117.2 1.3 fusion
  118.5 0.7 fusion.47
  119.2 0.8 multiply_reduce_fusion
  120.0 0.9 fusion.27
  120.9 13.4 %all_gather.11 = bf16[8,32,256]{2,1,0:T(8,128)(2,1)S(1)} all-gather(bf16[2,32,256]{2,1,0:T(8,128)(2,1)S(1)} %fusion.27), channel_id=1, replica_groups=mesh['rep'=8,'own'=4] {'own'}, dimensions={0}, use_global_device_ids=true | all-gather | bytes 163840 | tf_op jit(solution)/shard_map/all_gather | solution.py:88
  134.3 1.2 gather_fusion.1
  (9 shorter events, 0.1 us)
Async XLA Ops:
  7.2 1.8 %copy-start = (bf16[1,1,4,256,256]{4,3,2,1,0:T(8,128)(2,1)S(1)}, bf16[1,1,4,256,256]{4,3,2,1,0:T(8,128)(2,1)}, u32[]{:S(2)}) copy-start(bf16[1,1,4,256,256]{4,3,2,1,0:T(8,128)(2,1)} %param.9) | copy-start | bytes 1572868
  7.2 50.6 %reduce-scatter.2.cloned.1.call-start = ((), (), s32[]{:S(2)}) async-start(), calls=%async_computation.1 | async-start | bytes 2621440 | tf_op jit(solution)/shard_map/reduce_scatter | solution.py:64
  11.2 46.6 %copy-start.5 = (bf16[2,256,256]{2,1,0:T(8,128)(2,1)S(1)}, bf16[2,256,256]{2,1,0:T(8,128)(2,1)}, u32[]{:S(2)}) copy-start(bf16[2,256,256]{2,1,0:T(8,128)(2,1)} %param.13) | copy-start | bytes 786436
  11.2 46.7 %copy-start.6 = (bf16[2,256,256]{2,1,0:T(8,128)(2,1)S(1)}, bf16[2,256,256]{2,1,0:T(8,128)(2,1)}, u32[]{:S(2)}) copy-start(bf16[2,256,256]{2,1,0:T(8,128)(2,1)} %param.14) | copy-start | bytes 786436
  11.3 84.2 %all-gather.3.cloned.1.call-start = ((), (), s32[]{:S(2)}) async-start(), calls=%async_computation.2 | async-start | bytes 4718592 | tf_op jit(solution)/shard_map/all_gather | solution.py:65
  95.5 2.6 %copy-start.1 = (f32[2,256,256]{2,1,0:T(8,128)S(1)}, f32[2,256,256]{2,1,0:T(8,128)}, u32[]{:S(2)}) copy-start(f32[2,256,256]{2,1,0:T(8,128)} %param.11) | copy-start | bytes 1572868
  98.1 1.0 copy-start.2
  98.1 1.2 copy-start.3
  98.1 1.3 copy-start.4
Sparse Core Ops, SparseCore 0:
  11.4 46.3 reduce-scatter.1
  59.6 35.7 all-gather.2
